TPU v7x, 32 devices: a whole 2x2x4 slice. The times are simulated.
32 devices in a mesh: dp: 8 (over z, y), expert: 4 (over x, core).
Axes of the slice: x: 2, y: 2, z: 4, core: 2. Of those that a mesh axis runs over, the one named last changes fastest.
Arguments:
- tokens: bfloat16 [4, 1024, 1536], P('expert', 'dp'), may hold values from -6 to 6
- cotangent: bfloat16 [4, 1024, 1536], P('expert', 'dp'), may hold values from -6 to 6
- lengths: int32 [4, 2], P('expert'), may hold values from 341 to 683, as said below
- deal: int32 [4], replicated, may hold values from 0 to 3, each once
- routes: int32 [4, 1024, 8], P('expert', 'dp'), may hold values from 0 to 39, all different within a row; in each aligned block of 128 rows (0 to 127, 128 to 255, ..., all dimensions but the last counted through in order) at most 40 rows name the same one
- gates: float32 [4, 1024, 8], P('expert', 'dp'), may hold values from 0.15 to 0.5
- q_weight: float32 [1536, 1536], P(('dp', 'expert')), may hold values from -0.625 to 0.625
- k_weight: float32 [1536, 512], P(('dp', 'expert')), may hold values from -0.625 to 0.625
- v_weight: float32 [1536, 512], P(('dp', 'expert')), may hold values from -0.15625 to 0.15625
- o_weight: float32 [1536, 1536], P(('dp', 'expert')), may hold values from -1.5 to 1.5
- gain_attn: float32 [1536], P(('dp', 'expert')), may hold values from 0.5 to 1.5
- gain_moe: float32 [1536], P(('dp', 'expert')), may hold values from 0.5 to 1.5
- in_weight: float32 [1536, 40, 1024], P('dp', 'expert'), may hold values from -0.15625 to 0.15625
- down_weight: float32 [512, 40, 1536], P('dp', 'expert'), may hold values from -1 to 1
Outputs:
- output: float32 [4, 1024, 1536], P('expert', 'dp')
- input_grad: float32 [4, 1024, 1536], P('expert', 'dp')
- q_weight_grad: float32 [1536, 1536], P(('dp', 'expert'))
- k_weight_grad: float32 [1536, 512], P(('dp', 'expert'))
- v_weight_grad: float32 [1536, 512], P(('dp', 'expert'))
- o_weight_grad: float32 [1536, 1536], P(('dp', 'expert'))
- gain_attn_grad: float32 [1536], P(('dp', 'expert'))
- gain_moe_grad: float32 [1536], P(('dp', 'expert'))
- in_weight_grad: float32 [1536, 40, 1024], P('dp', 'expert')
- down_weight_grad: float32 [512, 40, 1536], P('dp', 'expert')
Inputs may be any that keep to these rules, and one draw needn't show every extreme that they name: In each group the lengths of sequences 2i and 2i + 1 sum to 1024; in some group a sequence has the largest length. `routes`: each token names 8 different experts; in the rows of one device no expert is named by more than 40 rows.
All inputs are finite; a program needn't handle non-finite values.
Results may differ from a plain program's by a relative error of at most 0.018.
The roundings to bfloat16 on the way count: a program that leaves them out, or rounds other values in their place, can miss the bound.
Values may be sent and summed in bfloat16 or wider, within the bound.
No kernel may reach another device: no remote copies, remote signals or barrier semaphores. Data moves between devices by JAX's collectives and lax.ppermute only.
A program may use at most 256 MiB of HBM per device.

v0:
```python
import jax
import jax.numpy as jnp
from jax import lax
from jax.sharding import PartitionSpec as P

H = 24
KVH = 8
HD = 64
E = 40
FF = 512
TOPK = 8
CAP = 40


EPSILON = 1e-06
RESIDUAL = 0.22
SCORE_SCALE = 0.015625
THETA = 10000.0
NEGATIVE = -1e30
ROWS_DIMS = (((0,), (0,)), ((), ()))
COLS_DIMS = (((1,), (1,)), ((), ()))


def rms_scale(values, gain):
    return values * lax.rsqrt(jnp.mean(values * values, axis=-1, keepdims=True) + EPSILON) * gain


def rotate(values, cosine, sine_table):
    half_width = values.shape[-1] // 2
    turned = jnp.concatenate([-values[..., half_width:], values[..., :half_width]], axis=-1)
    return values * cosine + turned * sine_table


def turn_back(grads_in, cosine, sine_table):
    half_width = grads_in.shape[-1] // 2
    scaled = grads_in * sine_table
    return grads_in * cosine + jnp.concatenate(
        [scaled[..., half_width:], -scaled[..., :half_width]], axis=-1
    )


def silu_product(gate_in, up_in):
    return jax.nn.silu(gate_in) * up_in


def locate(where_at, seq_ends):
    return jnp.sum((where_at[:, None] >= seq_ends[None, :]).astype(jnp.int32), axis=-1)


def cut_block(source, begin_at, block_rows, heads):
    piece = lax.dynamic_slice_in_dim(source, begin_at, block_rows, 0)
    return piece.reshape(block_rows, heads, source.shape[1] // heads)


def group_chooser(wanted, carried, pieces, start):
    piece_rows = pieces[0].shape[0]
    inside = (wanted >= start) & (wanted < start + piece_rows)
    offset_at = jnp.clip(wanted, 0, piece_rows - 1)
    return tuple(
        (
            jnp.where(inside, lax.dynamic_slice_in_dim(member_piece, offset_at, 1, 0), member_carry)
            for member_piece, member_carry in zip(pieces, carried)
        )
    )


def per_device(
    tokens,
    cotangent,
    lengths,
    deal,
    routes,
    gates,
    q_weight,
    k_weight,
    v_weight,
    o_weight,
    gain_attn,
    gain_moe,
    in_weight,
    down_weight,
):
    tok_rows = tokens.shape[1]
    model_width = tokens.shape[2]
    group_rows = tok_rows * lax.axis_size("dp")
    block_rows = min(512, group_rows)
    heads_per = H // KVH
    owner_index = lax.axis_index("expert")
    group_ids = jnp.arange(deal.shape[0], dtype=jnp.int32)
    wanted_in = jnp.sum(jnp.where(group_ids == owner_index, deal, 0))
    wanted_out = jnp.sum(jnp.where(deal == owner_index, group_ids, 0))
    dealt_tokens, dealt_cotangent = group_chooser(
        wanted_in,
        (jnp.zeros_like(tokens), jnp.zeros_like(cotangent)),
        (
            lax.all_gather(tokens, "expert", axis=0, tiled=True),
            lax.all_gather(cotangent, "expert", axis=0, tiled=True),
        ),
        jnp.int32(0),
    )
    inputs = dealt_tokens[0].astype(jnp.float32)
    q_full, k_full, v_full, o_full, gain_one, gain_two = (
        lax.all_gather(q_weight.astype(jnp.bfloat16), ("dp", "expert"), axis=0, tiled=True),
        lax.all_gather(k_weight.astype(jnp.bfloat16), ("dp", "expert"), axis=0, tiled=True),
        lax.all_gather(v_weight.astype(jnp.bfloat16), ("dp", "expert"), axis=0, tiled=True),
        lax.all_gather(o_weight.astype(jnp.bfloat16), ("dp", "expert"), axis=0, tiled=True),
        lax.all_gather(gain_attn.astype(jnp.bfloat16), ("dp", "expert"), axis=0, tiled=True),
        lax.all_gather(gain_moe.astype(jnp.bfloat16), ("dp", "expert"), axis=0, tiled=True),
    )
    gain_one = gain_one.astype(jnp.float32)
    gain_two = gain_two.astype(jnp.float32)
    seq_lengths = lengths[0]
    seq_ends = jnp.cumsum(seq_lengths)
    seq_starts = seq_ends - seq_lengths
    first_place = lax.axis_index("dp") * tok_rows
    places = first_place + jnp.arange(tok_rows, dtype=jnp.int32)
    member = (places[:, None] >= seq_starts[None, :]) & (places[:, None] < seq_ends[None, :])
    offsets = jnp.sum(jnp.where(member, places[:, None] - seq_starts[None, :], 0), axis=-1)
    frequency = THETA ** (-jnp.arange(HD // 2, dtype=jnp.float32) * 2.0 / HD)
    angles = offsets.astype(jnp.float32)[:, None] * frequency[None, :]
    angles = jnp.concatenate([angles, angles], axis=-1)[:, None, :]
    cosine = jnp.cos(angles)
    sine_table = jnp.sin(angles)
    query_seq = locate(places, seq_ends)
    seq_floor = jnp.sum(jnp.where(member[0], seq_starts, 0))
    low_block = seq_floor // block_rows
    high_block = (first_place + tok_rows - 1) // block_rows + 1
    normed = rms_scale(inputs, gain_one).astype(jnp.bfloat16)
    query_pre = jnp.dot(normed, q_full, preferred_element_type=jnp.float32).reshape(tok_rows, H, HD)
    key_pre = jnp.dot(normed, k_full, preferred_element_type=jnp.float32).reshape(tok_rows, KVH, HD)
    value_rows = jnp.dot(normed, v_full, preferred_element_type=jnp.float32).astype(jnp.bfloat16)
    queries = (
        rotate(query_pre, cosine, sine_table)
        .astype(jnp.bfloat16)
        .reshape(tok_rows, KVH, heads_per, HD)
    )
    key_rows = rotate(key_pre, cosine, sine_table).astype(jnp.bfloat16).reshape(tok_rows, KVH * HD)
    all_keys, all_values = (
        lax.all_gather(key_rows, "dp", axis=0, tiled=True),
        lax.all_gather(value_rows, "dp", axis=0, tiled=True),
    )

    def scores_for(block_id, key_block):
        begin_at = block_id * block_rows
        key_places = begin_at + jnp.arange(block_rows, dtype=jnp.int32)
        allowed = (query_seq[:, None] == locate(key_places, seq_ends)[None, :]) & (
            key_places[None, :] <= places[:, None]
        )
        raw_scores = SCORE_SCALE * jnp.einsum(
            "tkgd,skd->kgts", queries, key_block, preferred_element_type=jnp.float32
        )
        return (raw_scores, allowed)

    def stats_step(block_id, carried):
        run_top, run_total = carried
        key_block = cut_block(all_keys, block_id * block_rows, block_rows, KVH)
        raw_scores, allowed = scores_for(block_id, key_block)
        new_top = jnp.maximum(run_top, jnp.max(jnp.where(allowed, raw_scores, NEGATIVE), axis=-1))
        weights_now = jnp.where(allowed, jnp.exp(raw_scores - new_top[..., None]), 0.0)
        run_total = run_total * jnp.exp(run_top - new_top) + jnp.sum(weights_now, axis=-1)
        return (new_top, run_total)

    top_init = jnp.full((KVH, heads_per, tok_rows), NEGATIVE, jnp.float32)
    total_init = jnp.zeros((KVH, heads_per, tok_rows), jnp.float32)
    run_top, run_total = lax.fori_loop(low_block, high_block, stats_step, (top_init, total_init))
    log_total = run_top + jnp.log(run_total)

    def attn_probs(block_id, key_block):
        raw_scores, allowed = scores_for(block_id, key_block)
        return jnp.where(allowed, jnp.exp(raw_scores - log_total[..., None]), 0.0)

    def value_step(block_id, running):
        key_block = cut_block(all_keys, block_id * block_rows, block_rows, KVH)
        value_block = cut_block(all_values, block_id * block_rows, block_rows, KVH)
        chances = attn_probs(block_id, key_block).astype(jnp.bfloat16)
        return running + jnp.einsum(
            "kgts,skd->tkgd", chances, value_block, preferred_element_type=jnp.float32
        )

    mixed_init = jnp.zeros((tok_rows, KVH, heads_per, HD), jnp.float32)
    mixed_rows = lax.fori_loop(low_block, high_block, value_step, mixed_init).reshape(
        tok_rows, H * HD
    )
    mixed_low = mixed_rows.astype(jnp.bfloat16)
    branch = lax.dot_general(mixed_low, o_full, COLS_DIMS, preferred_element_type=jnp.float32)
    middle = inputs + RESIDUAL * branch
    sent_rows = rms_scale(middle, gain_two).astype(jnp.bfloat16)
    route_ids = routes[0].reshape(tok_rows * TOPK)
    matches = (route_ids[:, None] == jnp.arange(E, dtype=jnp.int32)[None, :]).astype(jnp.int32)
    slot_rank = jnp.sum(matches * jnp.cumsum(matches, axis=0), axis=-1) - 1
    slot_index = route_ids * CAP + slot_rank
    copies = jnp.repeat(sent_rows, TOPK, axis=0)
    outgoing = (
        jnp.zeros((E * CAP, model_width), jnp.bfloat16)
        .at[slot_index]
        .set(copies)
        .reshape(E, CAP, model_width)
    )
    arrived = lax.all_to_all(outgoing, "expert", split_axis=0, concat_axis=1, tiled=True)
    w_in, w_down = (
        lax.all_gather(in_weight.astype(jnp.bfloat16), "dp", axis=0, tiled=True),
        lax.all_gather(down_weight.astype(jnp.bfloat16), "dp", axis=0, tiled=True),
    )
    gate_up = jnp.einsum("erd,def->erf", arrived, w_in, preferred_element_type=jnp.float32)
    gate_part = gate_up[..., :FF]
    up_part = gate_up[..., FF:]
    hidden = silu_product(gate_part, up_part).astype(jnp.bfloat16)
    produced = jnp.einsum(
        "erf,fed->erd", hidden, w_down, preferred_element_type=jnp.float32
    ).astype(jnp.bfloat16)
    returned = lax.all_to_all(produced, "expert", split_axis=1, concat_axis=0, tiled=True).reshape(
        E * CAP, model_width
    )
    route_gates = gates[0].reshape(tok_rows * TOPK)
    picked = returned[slot_index].astype(jnp.float32) * route_gates[:, None]
    expert_sum = jnp.sum(picked.reshape(tok_rows, TOPK, model_width), axis=1)
    output = middle + RESIDUAL * expert_sum
    upstream = dealt_cotangent[0].astype(jnp.float32)
    spread = (RESIDUAL * route_gates[:, None] * jnp.repeat(upstream, TOPK, axis=0)).astype(
        jnp.bfloat16
    )
    back_out = (
        jnp.zeros((E * CAP, model_width), jnp.bfloat16)
        .at[slot_index]
        .set(spread)
        .reshape(E, CAP, model_width)
    )
    back_in = lax.all_to_all(back_out, "expert", split_axis=0, concat_axis=1, tiled=True)
    hidden_grad = jnp.einsum("erd,fed->erf", back_in, w_down, preferred_element_type=jnp.float32)
    down_term = jnp.einsum("erf,erd->fed", hidden, back_in, preferred_element_type=jnp.float32)
    ignored, silu_pull = jax.vjp(silu_product, gate_part, up_part)
    gate_grad, up_grad = silu_pull(hidden_grad)
    gate_up_grad = jnp.concatenate([gate_grad, up_grad], axis=-1).astype(jnp.bfloat16)
    in_term = jnp.einsum("erd,erf->def", arrived, gate_up_grad, preferred_element_type=jnp.float32)
    arrived_grad = jnp.einsum(
        "erf,def->erd", gate_up_grad, w_in, preferred_element_type=jnp.float32
    ).astype(jnp.bfloat16)
    sent_back = lax.all_to_all(
        arrived_grad, "expert", split_axis=1, concat_axis=0, tiled=True
    ).reshape(E * CAP, model_width)
    sent_grad = jnp.sum(
        sent_back[slot_index].astype(jnp.float32).reshape(tok_rows, TOPK, model_width), axis=1
    )
    in_grad, down_grad = (
        lax.psum_scatter(
            in_term.astype(jnp.bfloat16), "dp", scatter_dimension=0, tiled=True
        ).astype(jnp.float32),
        lax.psum_scatter(
            down_term.astype(jnp.bfloat16), "dp", scatter_dimension=0, tiled=True
        ).astype(jnp.float32),
    )
    ignored, second_pull = jax.vjp(rms_scale, middle, gain_two)
    middle_part, gain_two_term = second_pull(sent_grad)
    middle_grad = upstream + middle_part
    branch_grad = (RESIDUAL * middle_grad).astype(jnp.bfloat16)
    o_term = lax.dot_general(branch_grad, mixed_low, ROWS_DIMS, preferred_element_type=jnp.float32)
    grad_heads = jnp.dot(branch_grad, o_full, preferred_element_type=jnp.float32).astype(
        jnp.bfloat16
    )
    grad_heads = grad_heads.reshape(tok_rows, KVH, heads_per, HD)

    def delta_step(block_id, running):
        key_block = cut_block(all_keys, block_id * block_rows, block_rows, KVH)
        value_block = cut_block(all_values, block_id * block_rows, block_rows, KVH)
        chances = attn_probs(block_id, key_block)
        prob_grad = jnp.einsum(
            "tkgd,skd->kgts", grad_heads, value_block, preferred_element_type=jnp.float32
        )
        return running + jnp.sum(chances * prob_grad, axis=-1)

    row_delta = lax.fori_loop(
        low_block, high_block, delta_step, jnp.zeros((KVH, heads_per, tok_rows), jnp.float32)
    )

    def grad_step(block_id, carried):
        query_grad, key_buffer, value_buffer = carried
        begin_at = block_id * block_rows
        key_block = cut_block(all_keys, begin_at, block_rows, KVH)
        value_block = cut_block(all_values, begin_at, block_rows, KVH)
        chances = attn_probs(block_id, key_block)
        prob_grad = jnp.einsum(
            "tkgd,skd->kgts", grad_heads, value_block, preferred_element_type=jnp.float32
        )
        score_grad = (chances * (prob_grad - row_delta[..., None])).astype(jnp.bfloat16)
        query_grad = query_grad + SCORE_SCALE * jnp.einsum(
            "kgts,skd->tkgd", score_grad, key_block, preferred_element_type=jnp.float32
        )
        key_part = SCORE_SCALE * jnp.einsum(
            "kgts,tkgd->skd", score_grad, queries, preferred_element_type=jnp.float32
        )
        value_part = jnp.einsum(
            "kgts,tkgd->skd",
            chances.astype(jnp.bfloat16),
            grad_heads,
            preferred_element_type=jnp.float32,
        )
        key_buffer = lax.dynamic_update_slice_in_dim(
            key_buffer, key_part.reshape(block_rows, KVH * HD), begin_at, 0
        )
        value_buffer = lax.dynamic_update_slice_in_dim(
            value_buffer, value_part.reshape(block_rows, KVH * HD), begin_at, 0
        )
        return (query_grad, key_buffer, value_buffer)

    grad_init = (
        jnp.zeros((tok_rows, KVH, heads_per, HD), jnp.float32),
        jnp.zeros((group_rows, KVH * HD), jnp.float32),
        jnp.zeros((group_rows, KVH * HD), jnp.float32),
    )
    query_grad, key_buffer, value_buffer = lax.fori_loop(
        low_block, high_block, grad_step, grad_init
    )
    key_grad, value_grad = (
        lax.psum_scatter(
            key_buffer.astype(jnp.bfloat16), "dp", scatter_dimension=0, tiled=True
        ).astype(jnp.float32),
        lax.psum_scatter(
            value_buffer.astype(jnp.bfloat16), "dp", scatter_dimension=0, tiled=True
        ).astype(jnp.float32),
    )
    query_low = (
        turn_back(query_grad.reshape(tok_rows, H, HD), cosine, sine_table)
        .reshape(tok_rows, H * HD)
        .astype(jnp.bfloat16)
    )
    key_low = (
        turn_back(key_grad.reshape(tok_rows, KVH, HD), cosine, sine_table)
        .reshape(tok_rows, KVH * HD)
        .astype(jnp.bfloat16)
    )
    value_low = value_grad.astype(jnp.bfloat16)
    q_term = lax.dot_general(normed, query_low, ROWS_DIMS, preferred_element_type=jnp.float32)
    k_term = lax.dot_general(normed, key_low, ROWS_DIMS, preferred_element_type=jnp.float32)
    v_term = lax.dot_general(normed, value_low, ROWS_DIMS, preferred_element_type=jnp.float32)
    normed_grad = lax.dot_general(query_low, q_full, COLS_DIMS, preferred_element_type=jnp.float32)
    normed_grad = normed_grad + lax.dot_general(
        key_low, k_full, COLS_DIMS, preferred_element_type=jnp.float32
    )
    normed_grad = normed_grad + lax.dot_general(
        value_low, v_full, COLS_DIMS, preferred_element_type=jnp.float32
    )
    ignored, first_pull = jax.vjp(rms_scale, inputs, gain_one)
    input_part, gain_one_term = first_pull(normed_grad)
    input_grad = middle_grad + input_part
    q_grad, k_grad, v_grad, o_grad, gain_attn_grad, gain_moe_grad = (
        lax.psum_scatter(q_term, ("dp", "expert"), scatter_dimension=0, tiled=True),
        lax.psum_scatter(k_term, ("dp", "expert"), scatter_dimension=0, tiled=True),
        lax.psum_scatter(v_term, ("dp", "expert"), scatter_dimension=0, tiled=True),
        lax.psum_scatter(o_term, ("dp", "expert"), scatter_dimension=0, tiled=True),
        lax.psum_scatter(gain_one_term, ("dp", "expert"), scatter_dimension=0, tiled=True),
        lax.psum_scatter(gain_two_term, ("dp", "expert"), scatter_dimension=0, tiled=True),
    )
    given_output, given_input_grad = group_chooser(
        wanted_out,
        (
            jnp.zeros((1, tok_rows, model_width), jnp.float32),
            jnp.zeros((1, tok_rows, model_width), jnp.float32),
        ),
        (
            lax.all_gather(output[None].astype(jnp.bfloat16), "expert", axis=0, tiled=True).astype(
                jnp.float32
            ),
            lax.all_gather(
                input_grad[None].astype(jnp.bfloat16), "expert", axis=0, tiled=True
            ).astype(jnp.float32),
        ),
        jnp.int32(0),
    )
    return (
        given_output,
        given_input_grad,
        q_grad,
        k_grad,
        v_grad,
        o_grad,
        gain_attn_grad,
        gain_moe_grad,
        in_grad,
        down_grad,
    )


def solution(mesh):
    placed = (
        P("expert", "dp", None),
        P("expert", "dp", None),
        P("expert", None),
        P(),
        P("expert", "dp", None),
        P("expert", "dp", None),
        P(("dp", "expert"), None),
        P(("dp", "expert"), None),
        P(("dp", "expert"), None),
        P(("dp", "expert"), None),
        P(("dp", "expert")),
        P(("dp", "expert")),
        P("dp", "expert", None),
        P("dp", "expert", None),
    )
    return jax.shard_map(
        per_device,
        mesh=mesh,
        in_specs=placed,
        out_specs=(
            P("expert", "dp", None),
            P("expert", "dp", None),
            P(("dp", "expert"), None),
            P(("dp", "expert"), None),
            P(("dp", "expert"), None),
            P(("dp", "expert"), None),
            P(("dp", "expert")),
            P(("dp", "expert")),
            P("dp", "expert", None),
            P("dp", "expert", None),
        ),
        check_vma=False,
    )
```

profile of v0, /device:TPU:0, one launch (start us, length us, event | category | flops | bytes accessed | tf_op | source)
XLA Modules:
  0.0 3080.4 jit_solution(16079049636860872668)
XLA Ops:
  16.1 42.4 %all-reduce.5 = (bf16[1536]{0:T(1024)(128)(2,1)S(1)}, bf16[1536]{0:T(1024)(128)(2,1)S(1)}) all-reduce(bf16[1536]{0:T(1024)(128)(2,1)S(1)} %dynamic-update-slice, bf16[1536]{0:T(1024)(128)(2,1)S(1)} %dynamic-update-slice.1), channel_id=1, replica_groups=mesh['dp'=8,'expert'=4] {'dp','expert'}, use_global_device_ids=true, to_apply=%add | all-reduce | flops 3072 | bytes 12288
  60.4 30.5 all-gather.17.cloned.1.call-done
  90.9 2.6 convolution_convert_fusion.4
  95.9 52.3 %all-gather.21.cloned.1.call-done = bf16[1536,512]{1,0:T(8,128)(2,1)} async-done(((bf16[48,512]{1,0:T(8,128)(2,1)}), bf16[1536,512]{1,0:T(8,128)(2,1)}) %all-gather.21.cloned.1.call-update) | async-done | bytes 1572880 | tf_op jit(solution)/shard_map/all_gather | solution.py:104
  153.1 6.1 convert_element_type.231
  159.3 3.7 convert_element_type.233
  166.8 11.3 reduce-window.11
  180.0 8.8 scatter_custom_fusion.1
  188.8 5.2 all-to-all-start.2
  194.0 17.1 all-gather.19.cloned.1.call-done
  212.6 67.7 %all-gather.25.cloned.1.call-done = bf16[1536,1536]{1,0:T(8,128)(2,1)} async-done(((bf16[48,1536]{1,0:T(8,128)(2,1)}), bf16[1536,1536]{1,0:T(8,128)(2,1)}) %all-gather.25.cloned.1.call-update) | async-done | bytes 4718608 | tf_op jit(solution)/shard_map/all_gather | solution.py:103
  280.3 6.6 copy.95
  286.9 4.0 fusion.84
  291.1 29.5 all-gather.23.cloned.1.call-done
  320.6 3.8 while.50
  324.6 3.3 while.51
  328.0 58.7 %all-gather.27.cloned.1.call-done = bf16[1536,1536]{1,0:T(8,128)(2,1)} async-done(((bf16[48,1536]{1,0:T(8,128)(2,1)}), bf16[1536,1536]{1,0:T(8,128)(2,1)}) %all-gather.27.cloned.1.call-update) | async-done | bytes 4718608 | tf_op jit(solution)/shard_map/all_gather | solution.py:106
  386.7 4.2 multiply_reduce_fusion.2
  391.0 8.9 scatter_custom_fusion
  399.9 5.0 all-to-all-start
  404.9 5.1 copy.107
  410.0 50.9 %all-to-all-done = bf16[40,40,1536]{2,1,0:T(8,128)(2,1)} async-done(((bf16[40,40,1536]{2,1,0:T(8,128)(2,1)}), bf16[40,40,1536]{2,1,0:T(8,128)(2,1)}, u32[]{:S(2)}, u32[]{:S(2)}) %all-to-all-start) | async-done | bytes 4915232 | tf_op jit(solution)/shard_map/all_to_all | solution.py:199
  460.8 5.1 copy.102
  466.0 519.5 %all-gather.29.cloned.1.call-done = bf16[1536,10,1024]{2,0,1:T(8,128)(2,1)} async-done(((bf16[192,10,1024]{2,0,1:T(8,128)(2,1)}), bf16[1536,10,1024]{2,0,1:T(8,128)(2,1)}) %all-gather.29.cloned.1.call-update) | async-done | bytes 31457296 | tf_op jit(solution)/shard_map/all_gather | solution.py:201
  985.5 18.0 fusion.122
  1003.5 198.5 %all-gather.31.cloned.1.call-done = bf16[512,10,1536]{2,0,1:T(8,128)(2,1)} async-done(((bf16[64,10,1536]{2,0,1:T(8,128)(2,1)}), bf16[512,10,1536]{2,0,1:T(8,128)(2,1)}) %all-gather.31.cloned.1.call-update) | async-done | bytes 15728656 | tf_op jit(solution)/shard_map/all_gather | solution.py:202
  1202.0 13.2 fusion.52
  1215.2 18.0 convolution_convert_fusion.1
  1233.2 8.7 copy.108
  1241.9 5.8 all-to-all-start.3
  1247.7 8.7 convolution_convert_fusion.2
  1256.4 6.2 copy.103
  1262.6 72.6 %all-to-all-done.3 = bf16[10,160,1536]{2,0,1:T(8,128)(2,1)} async-done(((bf16[10,160,1536]{2,0,1:T(8,128)(2,1)}), bf16[10,160,1536]{2,0,1:T(8,128)(2,1)}, u32[]{:S(2)}, u32[]{:S(2)}) %all-to-all-start.3) | async-done | bytes 4915232 | tf_op jit(solution)/shard_map/all_to_all | solution.py:238
  1335.2 5.5 all-to-all-start.1
  1340.9 8.2 copy.109
  1349.1 79.2 %all-to-all-done.1 = bf16[10,160,1536]{2,0,1:T(8,128)(2,1)} async-done(((bf16[10,160,1536]{2,0,1:T(8,128)(2,1)}), bf16[10,160,1536]{2,0,1:T(8,128)(2,1)}, u32[]{:S(2)}, u32[]{:S(2)}) %all-to-all-start.1) | async-done | bytes 4915232 | tf_op jit(solution)/shard_map/all_to_all | solution.py:211
  1428.3 8.1 copy.104
  1436.4 10.7 gather_fusion.1
  1447.1 10.3 gather_fusion
  1457.4 7.6 convert_reduce_fusion
  1468.9 3.2 convolution_convert_fusion.3
  1472.3 3.4 while.52
  1478.8 8.4 while.53
  1493.8 4.9 fusion.123
  1498.7 64.2 %reduce-scatter.25.cloned.1.call-done = bf16[128,512]{1,0:T(8,128)(2,1)} async-done(((bf16[1024,512]{1,0:T(8,128)(2,1)}), bf16[128,512]{1,0:T(8,128)(2,1)}) %reduce-scatter.25.cloned.1.call-update) | async-done | bytes 131088
  1564.0 2.4 convolution_add_fusion.1
  1566.4 63.4 %reduce-scatter.27.cloned.1.call-done = bf16[128,512]{1,0:T(8,128)(2,1)} async-done(((bf16[1024,512]{1,0:T(8,128)(2,1)}), bf16[128,512]{1,0:T(8,128)(2,1)}) %reduce-scatter.27.cloned.1.call-update) | async-done | bytes 131088
  1634.2 10.9 convert_bitcast_fusion
  1645.1 30.5 copy.113
  1677.1 16.2 convolution_convert_fusion
  1693.3 37.4 %copy.135 = bf16[1536,10240]{1,0:T(8,128)(2,1)} copy(bf16[1536,10240]{0,1:T(8,128)(2,1)} %bitcast.396) | data formatting | bytes 62914560
  1732.1 2.3 fusion.115
  1737.1 5.0 fusion.88
  1743.1 5.0 fusion.96
  1750.0 48.8 %all-reduce.4 = (f32[1536]{0:T(1024)S(1)}, f32[1536]{0:T(1024)S(1)}) all-reduce(f32[1536]{0:T(1024)S(1)} %get-tuple-element.536, f32[1536]{0:T(1024)S(1)} %copy-done.23), channel_id=10, replica_groups=mesh['dp'=8,'expert'=4] {'dp','expert'}, use_global_device_ids=true, to_apply=%region_39.40.clone | all-reduce | flops 3072 | bytes 24576
  1803.9 275.6 %reduce-scatter.23.cloned.1.call-done = bf16[64,10,1536]{2,1,0:T(8,128)(2,1)} async-done(((bf16[512,10,1536]{2,1,0:T(8,128)(2,1)}), bf16[64,10,1536]{2,1,0:T(8,128)(2,1)}) %reduce-scatter.23.cloned.1.call-update) | async-done | bytes 1966096 | tf_op jit(solution)/shard_map/reduce_scatter | solution.py:248
  2079.5 5.0 copy.115
  2084.5 491.5 %reduce-scatter.29.cloned.1.call-done = bf16[192,10240]{1,0:T(8,128)(2,1)} async-done(((bf16[1536,10240]{1,0:T(8,128)(2,1)}), bf16[192,10240]{1,0:T(8,128)(2,1)}) %reduce-scatter.29.cloned.1.call-update) | async-done | bytes 3932176
  2575.9 7.2 copy.136
  2583.2 8.2 copy.114
  2591.3 91.8 %reduce-scatter.17.cloned.1.call-done = f32[48,512]{1,0:T(8,128)} async-done(((f32[1536,512]{1,0:T(8,128)}), f32[48,512]{1,0:T(8,128)}) %reduce-scatter.17.cloned.1.call-update) | async-done | bytes 98320 | tf_op jit(solution)/shard_map/reduce_scatter | solution.py:347
  2683.1 107.0 %reduce-scatter.19.cloned.1.call-done = f32[48,512]{1,0:T(8,128)} async-done(((f32[1536,512]{1,0:T(8,128)}), f32[48,512]{1,0:T(8,128)}) %reduce-scatter.19.cloned.1.call-update) | async-done | bytes 98320 | tf_op jit(solution)/shard_map/reduce_scatter | solution.py:348
  2790.1 141.7 %reduce-scatter.15.cloned.1.call-done = f32[48,1536]{1,0:T(8,128)} async-done(((f32[1536,1536]{1,0:T(8,128)}), f32[48,1536]{1,0:T(8,128)}) %reduce-scatter.15.cloned.1.call-update) | async-done | bytes 294928 | tf_op jit(solution)/shard_map/reduce_scatter | solution.py:346
  2931.8 141.5 %reduce-scatter.21.cloned.1.call-done = f32[48,1536]{1,0:T(8,128)} async-done(((f32[1536,1536]{1,0:T(8,128)}), f32[48,1536]{1,0:T(8,128)}) %reduce-scatter.21.cloned.1.call-update) | async-done | bytes 294928 | tf_op jit(solution)/shard_map/reduce_scatter | solution.py:349
  (231 shorter events, 70.3 us)
Async XLA Ops:
  7.2 88.1 %copy-start.30 = (s32[1,2]{1,0:T(1,128)S(1)}, s32[1,2]{1,0:T(1,128)}, u32[]{:S(2)}) copy-start(s32[1,2]{1,0:T(1,128)} %param.24) | copy-start | bytes 28
  7.2 52.0 %all-gather.15.cloned.1.call-start = ((), (), s32[]{:S(2)}) async-start(), calls=%async_computation.12 | async-start | bytes 1966080 | tf_op jit(solution)/shard_map/all_gather | solution.py:96
  7.9 82.9 %all-gather.17.cloned.1.call-start = ((), (), s32[]{:S(2)}) async-start(), calls=%async_computation.13 | async-start | bytes 1622016 | tf_op jit(solution)/shard_map/all_gather | solution.py:105
  9.5 138.6 %all-gather.21.cloned.1.call-start = ((), (), s32[]{:S(2)}) async-start(), calls=%async_computation.15 | async-start | bytes 1622016 | tf_op jit(solution)/shard_map/all_gather | solution.py:104
  11.1 167.8 %all-gather.33.cloned.1.call-start = ((), (), s32[]{:S(2)}) async-start(), calls=%async_computation.21 | async-start | bytes 1966080 | tf_op jit(solution)/shard_map/all_gather | solution.py:97
  11.7 199.4 %all-gather.19.cloned.1.call-start = ((), (), s32[]{:S(2)}) async-start(), calls=%async_computation.14 | async-start | bytes 1179648 | tf_op jit(solution)/shard_map/all_gather | solution.py:140
  58.5 228.4 %copy-start.17 = (f32[1536]{0:T(1024)}, f32[1536]{0:T(1024)S(1)}, u32[]{:S(2)}) copy-start(f32[1536]{0:T(1024)S(1)} %convert_element_type.211) | copy-start | bytes 18436
  60.4 91.2 %copy-start.28 = (f32[128]{0:T(128)}, f32[128]{0:T(128)S(1)}, u32[]{:S(2)}) copy-start(f32[128]{0:T(128)S(1)} %fusion.72) | copy-start | bytes 1540
  60.4 226.5 %copy-start.24 = (f32[128]{0:T(128)}, f32[128]{0:T(128)S(1)}, u32[]{:S(2)}) copy-start(f32[128]{0:T(128)S(1)} %fusion.104) | copy-start | bytes 1540
  60.4 91.9 %copy-start.22 = (f32[48,1536]{1,0:T(8,128)S(1)}, f32[48,1536]{1,0:T(8,128)}, u32[]{:S(2)}) copy-start(f32[48,1536]{1,0:T(8,128)} %param.31) | copy-start | bytes 884740
  93.5 186.8 %all-gather.25.cloned.1.call-start = ((), (), s32[]{:S(2)}) async-start(), calls=%async_computation.17 | async-start | bytes 4866048 | tf_op jit(solution)/shard_map/all_gather | solution.py:103
  95.2 225.4 %all-gather.23.cloned.1.call-start = ((), (), s32[]{:S(2)}) async-start(), calls=%async_computation.16 | async-start | bytes 1179648 | tf_op jit(solution)/shard_map/all_gather | solution.py:139
  95.8 195.1 %copy-start.13 = (f32[128,64]{0,1:T(8,128)}, f32[128,64]{0,1:T(8,128)S(1)}, u32[]{:S(2)}) copy-start(f32[128,64]{0,1:T(8,128)S(1)} %get-tuple-element.659) | copy-start | bytes 98308
  95.8 195.1 %copy-start.15 = (f32[128,64]{0,1:T(8,128)}, f32[128,64]{0,1:T(8,128)S(1)}, u32[]{:S(2)}) copy-start(f32[128,64]{0,1:T(8,128)S(1)} %get-tuple-element.660) | copy-start | bytes 98308
  152.3 234.4 %all-gather.27.cloned.1.call-start = ((), (), s32[]{:S(2)}) async-start(), calls=%async_computation.18 | async-start | bytes 4866048 | tf_op jit(solution)/shard_map/all_gather | solution.py:106
  153.0 832.5 %all-gather.29.cloned.1.call-start = ((), (), s32[]{:S(2)}) async-start(), calls=%async_computation.19 | async-start | bytes 35389440 | tf_op jit(solution)/shard_map/all_gather | solution.py:201
  159.2 7.1 copy-start.26
  159.2 19.2 copy-start.27
  159.2 1042.8 %all-gather.31.cloned.1.call-start = ((), (), s32[]{:S(2)}) async-start(), calls=%async_computation.20 | async-start | bytes 17694720 | tf_op jit(solution)/shard_map/all_gather | solution.py:202
  188.8 211.2 %all-to-all-start.2 = ((bf16[40,40,1536]{2,1,0:T(8,128)(2,1)}), bf16[40,40,1536]{2,1,0:T(8,128)(2,1)}, u32[]{:S(2)}, u32[]{:S(2)}) async-start(bf16[40,40,1536]{2,1,0:T(8,128)(2,1)} %bitcast.408), calls=%async_computation.2 | async-start | bytes 9830400 | tf_op jit(solution)/shard_map/all_to_all | solution.py:228
  328.0 72.0 %copy-start.10 = (bf16[128,8,3,64]{0,3,2,1:T(8,128)(2,1)}, bf16[128,8,3,64]{0,3,2,1:T(8,128)(2,1)S(1)}, u32[]{:S(2)}) copy-start(bf16[128,8,3,64]{0,3,2,1:T(8,128)(2,1)S(1)} %convert_element_type.224) | copy-start | bytes 1179652
  399.9 60.9 %all-to-all-start = ((bf16[40,40,1536]{2,1,0:T(8,128)(2,1)}), bf16[40,40,1536]{2,1,0:T(8,128)(2,1)}, u32[]{:S(2)}, u32[]{:S(2)}) async-start(bf16[40,40,1536]{2,1,0:T(8,128)(2,1)} %bitcast.409), calls=%async_computation | async-start | bytes 9830400 | tf_op jit(solution)/shard_map/all_to_all | solution.py:199
  1241.9 93.3 %all-to-all-start.3 = ((bf16[10,160,1536]{2,0,1:T(8,128)(2,1)}), bf16[10,160,1536]{2,0,1:T(8,128)(2,1)}, u32[]{:S(2)}, u32[]{:S(2)}) async-start(bf16[10,160,1536]{2,0,1:T(8,128)(2,1)} %copy.108), calls=%async_computation.3 | async-start | bytes 15728640 | tf_op jit(solution)/shard_map/all_to_all | solution.py:238
  1335.2 93.1 %all-to-all-start.1 = ((bf16[10,160,1536]{2,0,1:T(8,128)(2,1)}), bf16[10,160,1536]{2,0,1:T(8,128)(2,1)}, u32[]{:S(2)}, u32[]{:S(2)}) async-start(bf16[10,160,1536]{2,0,1:T(8,128)(2,1)} %copy.103), calls=%async_computation.1 | async-start | bytes 15728640 | tf_op jit(solution)/shard_map/all_to_all | solution.py:211
  1340.8 222.1 %reduce-scatter.25.cloned.1.call-start = ((), (), s32[]{:S(2)}) async-start(), calls=%async_computation.29 | async-start | bytes 1179648
  1465.9 6.4 copy-start
  1468.0 0.9 copy-start.1
  1475.8 0.7 copy-start.20
  1478.8 1.4 copy-start.21
  1483.0 2.5 copy-start.6
  1483.1 2.5 copy-start.8
  1485.7 1.0 copy-start.7
  1485.7 1.3 copy-start.9
  1487.2 4.7 copy-start.16
  1487.2 5.5 copy-start.14
  1489.5 140.3 %reduce-scatter.27.cloned.1.call-start = ((), (), s32[]{:S(2)}) async-start(), calls=%async_computation.30 | async-start | bytes 1179648
  1491.9 308.1 %all-gather.35.cloned.1.call-start = ((), (), s32[]{:S(2)}) async-start(), calls=%async_computation.27 | async-start | bytes 1966080 | tf_op jit(solution)/shard_map/all_gather | solution.py:360
  1492.6 309.3 %all-gather.37.cloned.1.call-start = ((), (), s32[]{:S(2)}) async-start(), calls=%async_computation.28 | async-start | bytes 1966080 | tf_op jit(solution)/shard_map/all_gather | solution.py:363
  1493.7 136.1 %copy-start.18 = (f32[1536]{0:T(1024)S(1)}, f32[1536]{0:T(1024)}, u32[]{:S(2)}) copy-start(f32[1536]{0:T(1024)} %copy-done.17) | copy-start | bytes 18436
  1493.8 136.1 %copy-start.25 = (f32[128]{0:T(128)S(1)}, f32[128]{0:T(128)}, u32[]{:S(2)}) copy-start(f32[128]{0:T(128)} %copy-done.24) | copy-start | bytes 1540
  1498.7 133.4 %copy-start.29 = (f32[128]{0:T(128)S(1)}, f32[128]{0:T(128)}, u32[]{:S(2)}) copy-start(f32[128]{0:T(128)} %copy-done.28) | copy-start | bytes 1540
  1498.7 133.5 %copy-start.2 = (f32[128,1536]{1,0:T(8,128)S(1)}, f32[128,1536]{1,0:T(8,128)}, u32[]{:S(2)}) copy-start(f32[128,1536]{1,0:T(8,128)} %copy-done.1) | copy-start | bytes 2359300
  1564.0 70.2 %copy-start.3 = (bf16[10,160,512]{2,1,0:T(8,128)(2,1)S(1)}, bf16[10,160,512]{2,1,0:T(8,128)(2,1)}, u32[]{:S(2)}) copy-start(bf16[10,160,512]{2,1,0:T(8,128)(2,1)} %get-tuple-element.646) | copy-start | bytes 4915204
  1634.2 445.4 %reduce-scatter.23.cloned.1.call-start = ((), (), s32[]{:S(2)}) async-start(), calls=%async_computation.26 | async-start | bytes 28311552 | tf_op jit(solution)/shard_map/reduce_scatter | solution.py:248
  1675.7 1.4 copy-start.4
  1675.7 900.2 %reduce-scatter.29.cloned.1.call-start = ((), (), s32[]{:S(2)}) async-start(), calls=%async_computation.31 | async-start | bytes 35389440
  1730.7 1.4 copy-start.5
  1730.7 3.8 copy-start.19
  1730.7 952.4 %reduce-scatter.17.cloned.1.call-start = ((), (), s32[]{:S(2)}) async-start(), calls=%async_computation.23 | async-start | bytes 3244032 | tf_op jit(solution)/shard_map/reduce_scatter | solution.py:347
  1734.4 2.7 copy-start.12
  1734.4 1055.7 %reduce-scatter.19.cloned.1.call-start = ((), (), s32[]{:S(2)}) async-start(), calls=%async_computation.24 | async-start | bytes 3244032 | tf_op jit(solution)/shard_map/reduce_scatter | solution.py:348
  1736.8 1195.0 %reduce-scatter.15.cloned.1.call-start = ((), (), s32[]{:S(2)}) async-start(), calls=%async_computation.22 | async-start | bytes 9732096 | tf_op jit(solution)/shard_map/reduce_scatter | solution.py:346
  1742.1 1.0 copy-start.11
  1742.2 1331.1 %reduce-scatter.21.cloned.1.call-start = ((), (), s32[]{:S(2)}) async-start(), calls=%async_computation.25 | async-start | bytes 9732096 | tf_op jit(solution)/shard_map/reduce_scatter | solution.py:349
  1748.1 1.9 copy-start.23
Sparse Core Ops, SparseCore 0:
  9.6 22.8 all-gather.14
  35.9 54.9 all-gather.16
  94.3 53.8 all-gather.20
  149.6 18.6 all-gather.32
  170.8 40.2 all-gather.18
  214.4 65.7 all-gather.24
  282.9 37.6 all-gather.22
  324.1 62.5 all-gather.26
  388.8 596.6 all-gather.28
  987.5 214.4 all-gather.30
  1489.6 73.1 reduce-scatter.24
  1566.7 63.0 reduce-scatter.26
  1631.4 18.5 all-gather.34
  1651.9 19.6 all-gather.36
  1675.8 403.6 reduce-scatter.22
  2083.3 492.6 reduce-scatter.28
  2581.8 101.2 reduce-scatter.16
  2689.0 101.0 reduce-scatter.18
  2796.6 135.2 reduce-scatter.14
  2938.1 135.1 reduce-scatter.20
where the time goes:
time: 3090 us; the launch traced here: 3080 us
  waiting for transfers between devices  2560 us (83%)
  local copies, waits for them, and re-layouts  189 us (6%)
  matrix products  137 us (4%)
  blocking collectives  91.2 us (3%)
  other arithmetic  63.1 us (2%)
    unnamed x23, waiting for transfers between devices  621 us
    all_gather x1, waiting for transfers between devices, per_device(): lax.all_gather(in_weight.astype(jnp.bfloat16), 'dp', axis=0, tiled=True)  520 us
    reduce_scatter x1, waiting for transfers between devices, per_device(): lax.psum_scatter(down_term.astype(jnp.bfloat16), 'dp', scatter_dimension=...  276 us
    all_gather x1, waiting for transfers between devices, per_device(): lax.all_gather(down_weight.astype(jnp.bfloat16), 'dp', axis=0, tiled=True)  199 us
    reduce_scatter x1, waiting for transfers between devices, per_device(): lax.psum_scatter(q_term, ('dp', 'expert'), scatter_dimension=0, tiled=True)  142 us
    reduce_scatter x1, waiting for transfers between devices, per_device(): lax.psum_scatter(o_term, ('dp', 'expert'), scatter_dimension=0, tiled=True)  141 us
    reduce_scatter x1, waiting for transfers between devices, per_device(): lax.psum_scatter(v_term, ('dp', 'expert'), scatter_dimension=0, tiled=True)  107 us
    reduce_scatter x1, waiting for transfers between devices, per_device(): lax.psum_scatter(k_term, ('dp', 'expert'), scatter_dimension=0, tiled=True)  91.8 us
  transfers between devices with their start and end apart: 24, of which 19 were waited for; matrix products, arithmetic and copies ran while one was open for 9% of the time, Pallas kernels for 0%

commit v1 on v0

--- a/solution.py
+++ b/solution.py
@@ -64,7 +64,7 @@
     )
 
 
-def per_device(
+def per_device_wide(
     tokens,
     cotangent,
     lengths,
@@ -380,6 +380,320 @@
     )
 
 
+def rounded(values):
+    return lax.reduce_precision(values, 8, 7)
+
+
+def rope_parts(seq_lengths, rows):
+    seq_ends = jnp.cumsum(seq_lengths)
+    seq_starts = seq_ends - seq_lengths
+    places = jnp.arange(rows, dtype=jnp.int32)
+    member = (places[:, None] >= seq_starts[None, :]) & (places[:, None] < seq_ends[None, :])
+    offsets = jnp.sum(jnp.where(member, places[:, None] - seq_starts[None, :], 0), axis=-1)
+    frequency = THETA ** (-jnp.arange(HD // 2, dtype=jnp.float32) * 2.0 / HD)
+    angles = offsets.astype(jnp.float32)[:, None] * frequency[None, :]
+    angles = jnp.concatenate([angles, angles], axis=-1)[:, None, :]
+    seq_ids = locate(places, seq_ends)
+    return places, seq_ids, jnp.cos(angles), jnp.sin(angles)
+
+
+def per_device(
+    tokens,
+    cotangent,
+    lengths,
+    deal,
+    routes,
+    gates,
+    q_weight,
+    k_weight,
+    v_weight,
+    o_weight,
+    gain_attn,
+    gain_moe,
+    in_weight,
+    down_weight,
+):
+    n_dp = lax.axis_size("dp")
+    n_ex = lax.axis_size("expert")
+    tok_rows = tokens.shape[1]
+    model = tokens.shape[2]
+    group_rows = tok_rows * n_dp
+    kv_here = KVH // n_dp
+    heads_per = H // KVH
+    q_cols = kv_here * heads_per * HD
+    kv_cols = kv_here * HD
+    own_experts = in_weight.shape[1]
+    ff_here = FF // n_dp
+    ff_cols = own_experts * ff_here
+    w_rows = q_weight.shape[0]
+    both = ("dp", "expert")
+    ex_index = lax.axis_index("expert")
+    group_ids = jnp.arange(deal.shape[0], dtype=jnp.int32)
+    dealt_of = jnp.argmax((deal[None, :] == group_ids[:, None]).astype(jnp.int32), axis=1)
+    own_dealt = jnp.sum(jnp.where(deal == ex_index, group_ids, 0))
+
+    group_tokens = lax.all_gather(tokens[0], "dp", axis=0, tiled=True)
+
+    def by_owner(weight):
+        return weight.astype(jnp.bfloat16).reshape(w_rows, n_dp, weight.shape[1] // n_dp)
+
+    length_parts = jnp.stack([lengths[0] // 128, lengths[0] % 128]).reshape(-1).astype(jnp.bfloat16)
+    n_len = length_parts.shape[0]
+    extra = jnp.concatenate(
+        [
+            gain_attn.astype(jnp.bfloat16)[:, None],
+            gain_moe.astype(jnp.bfloat16)[:, None],
+            jnp.broadcast_to(length_parts[None, :], (w_rows, n_len)),
+            jnp.zeros((w_rows, 126 - n_len), jnp.bfloat16),
+        ],
+        axis=1,
+    )
+    attn_out = jnp.concatenate(
+        [
+            by_owner(q_weight),
+            by_owner(k_weight),
+            by_owner(v_weight),
+            by_owner(o_weight),
+            jnp.broadcast_to(extra[:, None, :], (w_rows, n_dp, 128)),
+        ],
+        axis=2,
+    ).transpose(1, 0, 2)
+    attn_in = lax.all_to_all(attn_out, "dp", split_axis=0, concat_axis=0, tiled=True)
+    attn_all = lax.all_gather(attn_in, "expert", axis=0)
+    attn_w = attn_all.transpose(1, 0, 2, 3).reshape(model, -1)
+    qkv_cols = q_cols + 2 * kv_cols
+    qkv_w = attn_w[:, :qkv_cols]
+    o_w = attn_w[:, qkv_cols : qkv_cols + q_cols]
+    side = attn_w[:, qkv_cols + q_cols :]
+    gain_one = side[:, 0].astype(jnp.float32)
+    gain_two = side[:, 1].astype(jnp.float32)
+    own_parts = lax.dynamic_index_in_dim(attn_all, own_dealt, 0, keepdims=False)[
+        0, 0, qkv_cols + q_cols + 2 : qkv_cols + q_cols + 2 + n_len
+    ].astype(jnp.int32)
+    seq_lengths = own_parts[: n_len // 2] * 128 + own_parts[n_len // 2 :]
+
+    gate_rows = gates[0]
+    gate_top = rounded(gate_rows)
+    gate_mid = rounded(gate_rows - gate_top)
+    gate_low = gate_rows - gate_top - gate_mid
+    meta = jnp.concatenate(
+        [
+            routes[0].astype(jnp.float32),
+            gate_top,
+            gate_mid,
+            gate_low,
+            jnp.zeros((tok_rows, 128 - 4 * TOPK), jnp.float32),
+        ],
+        axis=1,
+    ).astype(jnp.bfloat16)
+    cot_all = lax.all_gather(
+        jnp.concatenate([cotangent[0], meta], axis=1), both, axis=0, tiled=True
+    )
+
+    in_out = (
+        in_weight.astype(jnp.bfloat16)
+        .reshape(in_weight.shape[0], own_experts, 2, n_dp, ff_here)
+        .transpose(3, 0, 2, 1, 4)
+        .reshape(n_dp, in_weight.shape[0], 2 * ff_cols)
+    )
+    in_w = lax.all_to_all(in_out, "dp", split_axis=0, concat_axis=0, tiled=True).reshape(
+        model, 2 * ff_cols
+    )
+    down_w = down_weight.astype(jnp.bfloat16).transpose(1, 0, 2).reshape(ff_cols, model)
+
+    places, seq_ids, cosine, sine_table = rope_parts(seq_lengths, group_rows)
+    group_inputs = group_tokens.astype(jnp.float32)
+    first_scale = lax.rsqrt(jnp.mean(group_inputs * group_inputs, axis=-1, keepdims=True) + EPSILON)
+    normed = (group_inputs * first_scale * gain_one).astype(jnp.bfloat16)
+    qkv = jnp.dot(normed, qkv_w, preferred_element_type=jnp.float32)
+    queries = rotate(
+        qkv[:, :q_cols].reshape(group_rows, kv_here * heads_per, HD), cosine, sine_table
+    )
+    queries = queries.astype(jnp.bfloat16).reshape(group_rows, kv_here, heads_per, HD)
+    keys = rotate(
+        qkv[:, q_cols : q_cols + kv_cols].reshape(group_rows, kv_here, HD), cosine, sine_table
+    ).astype(jnp.bfloat16)
+    vals = qkv[:, q_cols + kv_cols :].astype(jnp.bfloat16).reshape(group_rows, kv_here, HD)
+    allowed = (seq_ids[:, None] == seq_ids[None, :]) & (places[None, :] <= places[:, None])
+    raw_scores = SCORE_SCALE * jnp.einsum(
+        "tkgd,skd->kgts", queries, keys, preferred_element_type=jnp.float32
+    )
+    chances = jax.nn.softmax(jnp.where(allowed, raw_scores, NEGATIVE), axis=-1)
+    chances_low = chances.astype(jnp.bfloat16)
+    mixed_low = (
+        jnp.einsum("kgts,skd->tkgd", chances_low, vals, preferred_element_type=jnp.float32)
+        .astype(jnp.bfloat16)
+        .reshape(group_rows, q_cols)
+    )
+    branch_part = lax.dot_general(mixed_low, o_w, COLS_DIMS, preferred_element_type=jnp.float32)
+    branch = lax.psum_scatter(
+        branch_part.astype(jnp.bfloat16), "dp", scatter_dimension=0, tiled=True
+    ).astype(jnp.float32)
+    inputs = tokens[0].astype(jnp.float32)
+    middle = inputs + RESIDUAL * branch
+    second_scale = lax.rsqrt(jnp.mean(middle * middle, axis=-1, keepdims=True) + EPSILON)
+    sent_rows = (middle * second_scale * gain_two).astype(jnp.bfloat16)
+    sent_all = lax.all_gather(sent_rows, both, axis=0, tiled=True)
+
+    meta_all = cot_all[:, model:].reshape(n_dp, n_ex, tok_rows, 128)
+    meta_all = jnp.take(meta_all, dealt_of, axis=1).reshape(-1, 128).astype(jnp.float32)
+    route_all = meta_all[:, :TOPK]
+    gate_all = (
+        meta_all[:, TOPK : 2 * TOPK]
+        + meta_all[:, 2 * TOPK : 3 * TOPK]
+        + meta_all[:, 3 * TOPK : 4 * TOPK]
+    )
+    expert_ids = (ex_index * own_experts + jnp.arange(own_experts, dtype=jnp.int32)).astype(
+        jnp.float32
+    )
+    dense_gates = jnp.sum(
+        jnp.where(route_all[:, :, None] == expert_ids[None, None, :], gate_all[:, :, None], 0.0),
+        axis=1,
+    )
+    gate_cols = jnp.repeat(dense_gates, ff_here, axis=1)
+    cot_rows = cot_all[:, :model]
+
+    gate_up = jnp.dot(sent_all, in_w, preferred_element_type=jnp.float32)
+    gate_part = gate_up[:, :ff_cols]
+    up_part = gate_up[:, ff_cols:]
+    sigma = jax.nn.sigmoid(gate_part)
+    silu = gate_part * sigma
+    hidden = (silu * up_part).astype(jnp.bfloat16).astype(jnp.float32)
+    weighted = (gate_cols * hidden).astype(jnp.bfloat16)
+    pulled = lax.dot_general(cot_rows, down_w, COLS_DIMS, preferred_element_type=jnp.float32)
+    hidden_grad = RESIDUAL * gate_cols * pulled
+    gate_grad = hidden_grad * up_part * (sigma * (1.0 + gate_part * (1.0 - sigma)))
+    up_grad = hidden_grad * silu
+    gate_up_grad = jnp.concatenate([gate_grad, up_grad], axis=1).astype(jnp.bfloat16)
+    sent_grad_part = lax.dot_general(
+        gate_up_grad, in_w, COLS_DIMS, preferred_element_type=jnp.float32
+    ).astype(jnp.bfloat16)
+    sent_grad = lax.psum_scatter(sent_grad_part, both, scatter_dimension=0, tiled=True).astype(
+        jnp.float32
+    )
+    out_part = jnp.dot(weighted, down_w, preferred_element_type=jnp.float32).astype(jnp.bfloat16)
+    expert_sum = lax.psum_scatter(out_part, both, scatter_dimension=0, tiled=True).astype(
+        jnp.float32
+    )
+    output = middle + RESIDUAL * expert_sum
+    in_term = lax.dot_general(sent_all, gate_up_grad, ROWS_DIMS, preferred_element_type=jnp.float32)
+    in_back = lax.all_to_all(
+        in_term.astype(jnp.bfloat16).reshape(n_dp, in_weight.shape[0], 2 * ff_cols),
+        "dp",
+        split_axis=0,
+        concat_axis=0,
+        tiled=True,
+    )
+    in_grad = (
+        in_back.reshape(n_dp, in_weight.shape[0], 2, own_experts, ff_here)
+        .transpose(1, 3, 2, 0, 4)
+        .reshape(in_weight.shape)
+        .astype(jnp.float32)
+    )
+    down_term = RESIDUAL * lax.dot_general(
+        weighted, cot_rows, ROWS_DIMS, preferred_element_type=jnp.float32
+    )
+    down_grad = down_term.reshape(own_experts, ff_here, model).transpose(1, 0, 2)
+
+    upstream = cotangent[0].astype(jnp.float32)
+    scaled_grad = sent_grad * gain_two
+    middle_grad = (
+        upstream
+        + second_scale * scaled_grad
+        - middle
+        * second_scale**3
+        * jnp.mean(scaled_grad * middle, axis=-1, keepdims=True)
+    )
+    gain_two_part = jnp.sum(sent_grad * middle * second_scale, axis=0)
+    branch_grad = (RESIDUAL * middle_grad).astype(jnp.bfloat16)
+    branch_grad_all = lax.all_gather(branch_grad, "dp", axis=0, tiled=True)
+
+    o_term = lax.dot_general(
+        branch_grad_all, mixed_low, ROWS_DIMS, preferred_element_type=jnp.float32
+    )
+    grad_heads = (
+        jnp.dot(branch_grad_all, o_w, preferred_element_type=jnp.float32)
+        .astype(jnp.bfloat16)
+        .reshape(group_rows, kv_here, heads_per, HD)
+    )
+    prob_grad = jnp.einsum(
+        "tkgd,skd->kgts", grad_heads, vals, preferred_element_type=jnp.float32
+    )
+    row_delta = jnp.sum(chances * prob_grad, axis=-1, keepdims=True)
+    score_grad = (chances * (prob_grad - row_delta)).astype(jnp.bfloat16)
+    query_grad = SCORE_SCALE * jnp.einsum(
+        "kgts,skd->tkgd", score_grad, keys, preferred_element_type=jnp.float32
+    )
+    key_grad = SCORE_SCALE * jnp.einsum(
+        "kgts,tkgd->skd", score_grad, queries, preferred_element_type=jnp.float32
+    )
+    value_grad = jnp.einsum(
+        "kgts,tkgd->skd", chances_low, grad_heads, preferred_element_type=jnp.float32
+    )
+    query_low = turn_back(
+        query_grad.reshape(group_rows, kv_here * heads_per, HD), cosine, sine_table
+    ).reshape(group_rows, q_cols)
+    key_low = turn_back(key_grad, cosine, sine_table).reshape(group_rows, kv_cols)
+    qkv_grad = jnp.concatenate(
+        [query_low, key_low, value_grad.reshape(group_rows, kv_cols)], axis=1
+    ).astype(jnp.bfloat16)
+    normed_grad_part = lax.dot_general(
+        qkv_grad, qkv_w, COLS_DIMS, preferred_element_type=jnp.float32
+    )
+    gain_one_part = jnp.sum(normed_grad_part * group_inputs * first_scale, axis=0)
+    normed_grad = lax.psum_scatter(
+        normed_grad_part.astype(jnp.bfloat16), "dp", scatter_dimension=0, tiled=True
+    ).astype(jnp.float32)
+    qkv_term = lax.dot_general(normed, qkv_grad, ROWS_DIMS, preferred_element_type=jnp.float32)
+    grads = jnp.concatenate(
+        [
+            qkv_term,
+            o_term,
+            gain_one_part[:, None],
+            gain_two_part[:, None],
+            jnp.zeros((model, 126), jnp.float32),
+        ],
+        axis=1,
+    ).astype(jnp.bfloat16)
+    grads = lax.psum_scatter(
+        grads.reshape(n_dp, n_ex, w_rows, -1).transpose(1, 0, 2, 3),
+        "expert",
+        scatter_dimension=0,
+        tiled=True,
+    )[0]
+    grads = lax.all_to_all(grads, "dp", split_axis=0, concat_axis=0, tiled=True).astype(jnp.float32)
+
+    def own_rows(begin, width):
+        return grads[:, :, begin : begin + width].transpose(1, 0, 2).reshape(w_rows, n_dp * width)
+
+    q_grad = own_rows(0, q_cols)
+    k_grad = own_rows(q_cols, kv_cols)
+    v_grad = own_rows(q_cols + kv_cols, kv_cols)
+    o_grad = own_rows(qkv_cols, q_cols)
+    gain_attn_grad = jnp.sum(grads[:, :, qkv_cols + q_cols], axis=0)
+    gain_moe_grad = jnp.sum(grads[:, :, qkv_cols + q_cols + 1], axis=0)
+
+    own_scale = lax.rsqrt(jnp.mean(inputs * inputs, axis=-1, keepdims=True) + EPSILON)
+    scaled_one = normed_grad * gain_one
+    input_grad = (
+        middle_grad
+        + own_scale * scaled_one
+        - inputs * own_scale**3 * jnp.mean(scaled_one * inputs, axis=-1, keepdims=True)
+    )
+    return (
+        output[None],
+        input_grad[None],
+        q_grad,
+        k_grad,
+        v_grad,
+        o_grad,
+        gain_attn_grad,
+        gain_moe_grad,
+        in_grad,
+        down_grad,
+    )
+
+
 def solution(mesh):
     placed = (
         P("expert", "dp", None),
@@ -397,8 +711,10 @@
         P("dp", "expert", None),
         P("dp", "expert", None),
     )
+    n_dp = mesh.shape["dp"]
+    split_heads = KVH % n_dp == 0 and (FF // n_dp) % 64 == 0
     return jax.shard_map(
-        per_device,
+        per_device if split_heads else per_device_wide,
         mesh=mesh,
         in_specs=placed,
         out_specs=(

time: 3090 us -> 1150 us (0.37)
  waiting for transfers between devices: 2560 us -> 779 us
  local copies, waits for them, and re-layouts: 189 us -> 80.3 us
  blocking collectives: 91.2 us -> 21 us
  matrix products: 137 us -> 174 us
    all_gather x12 -> x5, waiting for transfers between devices: 974 us -> 132 us  [the longest x1 58.2 us: per_device(): branch_grad_all = lax.all_gather(branch_grad, 'dp', axis=0, tiled=True)]
    unnamed x23 -> x11, waiting for transfers between devices: 621 us -> 5.05 us
    reduce_scatter x5 -> x4, waiting for transfers between devices: 758 us -> 413 us  [the longest x1 154 us: per_device(): lax.psum_scatter(sent_grad_part, both, scatter_dimension=0, tiled=True)]
    unnamed x2 -> x0, blocking collectives: 91.2 us -> none
    unnamed x67 -> x109, local copies, waits for them, and re-layouts: 71.8 us -> 23.1 us
    convert_element_type x4 -> x3, local copies, waits for them, and re-layouts: 45.7 us -> 4.95 us  [the longest x1 4.73 us: per_device(): in_grad = in_back.reshape(n_dp, in_weight.shape[0], 2, own_experts, ff_he...]
    dot_general x27 -> x18, matrix products: 137 us -> 174 us  [the longest x1 24 us: per_device(): lax.dot_general(gate_up_grad, in_w, COLS_DIMS, preferred_element_type=jnp...]
    all_to_all x4 -> x3, waiting for transfers between devices: 203 us -> 229 us  [the longest x1 124 us: per_device(): lax.all_to_all(in_out, 'dp', split_axis=0, concat_axis=0, tiled=True)]
  transfers between devices with their start and end apart: 24 -> 13, of which waited for: 19 -> 9; matrix products, arithmetic and copies ran while one was open for 9% -> 12% of each run, Pallas kernels for 0% -> 0%
where the time goes in v1:
time: 1150 us; the launch traced here: 1140 us
  waiting for transfers between devices  779 us (68%)
  matrix products  174 us (15%)
  local copies, waits for them, and re-layouts  80.3 us (7%)
  other arithmetic  51 us (4%)
  blocking collectives  21 us (2%)
  between operations  19.1 us (2%)
  starting transfers between devices  13.7 us (1%)
    reduce_scatter x1, waiting for transfers between devices, per_device(): lax.psum_scatter(sent_grad_part, both, scatter_dimension=0, tiled=True)  154 us
    reduce_scatter x1, waiting for transfers between devices, per_device(): lax.psum_scatter(out_part, both, scatter_dimension=0, tiled=True)  141 us
    all_to_all x1, waiting for transfers between devices, per_device(): lax.all_to_all(in_out, 'dp', split_axis=0, concat_axis=0, tiled=True)  124 us
    reduce_scatter x1, waiting for transfers between devices, per_device(): lax.psum_scatter(branch_part.astype(jnp.bfloat16), 'dp', scatter_dimensio...  119 us
    all_to_all x1, waiting for transfers between devices, per_device(): lax.all_to_all(in_term.astype(jnp.bfloat16).reshape(n_dp, in_weight.shape...  105 us
    all_gather x1, waiting for transfers between devices, per_device(): branch_grad_all = lax.all_gather(branch_grad, 'dp', axis=0, tiled=True)  58.2 us
    all_gather x1, waiting for transfers between devices, per_device(): group_tokens = lax.all_gather(tokens[0], 'dp', axis=0, tiled=True)  56 us
    dot_general x1, matrix products, per_device(): lax.dot_general(gate_up_grad, in_w, COLS_DIMS, preferred_element_type=jnp...  24 us
  transfers between devices with their start and end apart: 13, of which 9 were waited for; matrix products, arithmetic and copies ran while one was open for 12% of the time, Pallas kernels for 0%

profile of v1, /device:TPU:0, one launch (start us, length us, event | category | flops | bytes accessed | tf_op | source)
XLA Modules:
  0.0 1137.9 jit_solution(8235936435607646630)
XLA Ops:
  10.5 1.0 convert_element_type.195
  11.7 1.0 convert_element_type.198
  12.9 0.9 convert_element_type.196
  13.9 0.9 convert_element_type.197
  15.5 21.0 %all_to_all.20 = bf16[8,48,640]{2,1,0:T(8,128)(2,1)} all-to-all(bf16[8,48,640]{2,1,0:T(8,128)(2,1)S(1)} %copy.183), channel_id=1, replica_groups=mesh['dp'=8,'expert'=4] {'dp'}, dimensions={0} | all-to-all | bytes 983040 | tf_op jit(solution)/shard_map/all_to_all | solution.py:461
  40.0 17.6 %all-gather.16.cloned.1.call-done = bf16[32,48,640]{2,1,0:T(8,128)(2,1)} async-done(((bf16[8,48,640]{2,1,0:T(8,128)(2,1)}), bf16[32,48,640]{2,1,0:T(8,128)(2,1)}) %all-gather.16.cloned.1.call-update) | async-done | bytes 1966096 | tf_op jit(solution)/shard_map/all_gather | solution.py:462
  57.6 1.1 dynamic-slice_bitcast_fusion.1
  59.2 1.7 copy.184
  62.2 1.6 fusion.23
  63.8 56.0 %all-gather.14.cloned.1.call-done = bf16[1,1024,1536]{2,1,0:T(8,128)(2,1)} async-done(((bf16[1,128,1536]{2,1,0:T(8,128)(2,1)}), bf16[1,1024,1536]{2,1,0:T(8,128)(2,1)}) %all-gather.14.cloned.1.call-update) | async-done | bytes 3145744 | tf_op jit(solution)/shard_map/all_gather | solution.py:435
  119.8 2.6 fusion.13
  122.4 3.2 fusion.45
  125.9 1.0 fusion.69
  128.6 2.5 fusion.12
  131.1 4.4 fusion.4
  135.6 5.1 fusion.28
  141.5 4.3 convolution_convert_fusion.3
  147.6 118.5 %reduce-scatter.8.cloned.1.call-done = bf16[128,1536]{1,0:T(8,128)(2,1)} async-done(((bf16[1024,1536]{1,0:T(8,128)(2,1)}), bf16[128,1536]{1,0:T(8,128)(2,1)}) %reduce-scatter.8.cloned.1.call-update) | async-done | bytes 393232 | tf_op jit(solution)/shard_map/reduce_scatter | solution.py:529
  266.1 1.2 multiply_reduce_fusion
  267.4 1.9 multiply_convert_fusion.4
  269.3 8.6 copy.193
  277.9 5.7 copy.194
  283.6 7.4 copy.195
  291.0 4.5 all-to-all-start.1
  295.6 3.8 convert_element_type.229
  300.1 1.3 slice.147
  303.2 3.1 fusion.99
  306.2 2.2 copy.191
  309.4 123.8 %all-to-all-done.1 = bf16[8,192,1280]{2,1,0:T(8,128)(2,1)} async-done(((bf16[8,192,1280]{2,1,0:T(8,128)(2,1)}), bf16[8,192,1280]{2,1,0:T(8,128)(2,1)}, u32[]{:S(2)}, u32[]{:S(2)}) %all-to-all-start.1) | async-done | bytes 3932192 | tf_op jit(solution)/shard_map/all_to_all | solution.py:499
  433.3 22.7 %fusion.102 = f32[4096,1280]{0,1:T(8,128)} fusion(bf16[4096,1536]{1,0:T(8,128)(2,1)} %all-gather.10.cloned.1.call-done, bf16[1536,1280]{1,0:T(8,128)(2,1)} %bitcast.39), kind=kOutput, calls=%fused_computation.189 | convolution fusion | flops 16106127360 | bytes 37486592 | tf_op jit(solution)/shard_map/dot_general | solution.py:556
  455.9 22.8 %multiply_convert_fusion.1 = (bf16[4096,640]{0,1:T(8,128)(2,1)}, bf16[4096,640]{0,1:T(8,128)(2,1)}, bf16[4096,640]{0,1:T(8,128)(2,1)}) fusion(f32[4096,1280]{0,1:T(8,128)} %fusion.102, f32[4096,10]{0,1:T(8,128)S(1)} %select_reduce_fusion, bf16[640,1536]{1,0:T(8,128)(2,1)S(1)} %bitcast.273, bf16[4096,1664]{1,0:T(8,128)(2,1)} %all-gather.8.cloned.1.call-done), kind=kOutput, calls=%fused_computation.23 | convolution fusion | flops 8105492480 | bytes 51412992 | tf_op jit(solution)/shard_map/dot_general | solution.py:563
  478.7 24.0 %convolution_convert_fusion.1 = bf16[4096,1536]{1,0:T(8,128)(2,1)} fusion(bf16[1536,1280]{1,0:T(8,128)(2,1)} %bitcast.39, bf16[4096,640]{0,1:T(8,128)(2,1)} %get-tuple-element.92, bf16[4096,640]{0,1:T(8,128)(2,1)} %get-tuple-element.91), kind=kOutput, calls=%fused_computation.4 | convolution fusion | flops 16133390336 | bytes 27000832 | tf_op jit(solution)/shard_map/dot_general | solution.py:568
  502.8 153.8 %reduce-scatter.12.cloned.1.call-done = bf16[128,1536]{1,0:T(8,128)(2,1)} async-done(((bf16[4096,1536]{1,0:T(8,128)(2,1)}), bf16[128,1536]{1,0:T(8,128)(2,1)}) %reduce-scatter.12.cloned.1.call-update) | async-done | bytes 393232 | tf_op jit(solution)/shard_map/reduce_scatter | solution.py:571
  656.6 1.9 fusion.55
  658.5 2.1 multiply_convert_fusion.3
  661.4 58.2 %all-gather.12.cloned.1.call-done = bf16[1024,1536]{1,0:T(8,128)(2,1)} async-done(((bf16[128,1536]{1,0:T(8,128)(2,1)}), bf16[1024,1536]{1,0:T(8,128)(2,1)}) %all-gather.12.cloned.1.call-update) | async-done | bytes 3145744 | tf_op jit(solution)/shard_map/all_gather | solution.py:609
  719.6 3.6 convolution_convert_fusion.6
  723.3 10.3 fusion
  733.6 6.9 fusion.39
  740.6 7.2 fusion.18
  747.8 1.2 bitcast_multiply_fusion.5
  749.2 2.7 fusion.77
  753.6 2.3 convolution_convert_fusion.4
  756.0 1.8 copy.199
  757.8 4.8 copy.200
  762.6 6.1 fusion.17
  768.8 1.5 concatenate.95
  770.2 3.8 convolution_convert_fusion.5
  774.9 5.1 concatenate.94
  780.6 15.0 %convolution_convert_fusion = bf16[4096,1536]{1,0:T(8,128)(2,1)} fusion(bf16[4096,640]{0,1:T(8,128)(2,1)} %get-tuple-element.93, bf16[640,1536]{1,0:T(8,128)(2,1)S(1)} %bitcast.274), kind=kOutput, calls=%fused_computation.3 | convolution fusion | flops 8059355136 | bytes 19791872 | tf_op jit(solution)/shard_map/dot_general | solution.py:574
  795.6 23.4 %convolution_convert_fusion.2 = bf16[1536,1280]{1,0:T(8,128)(2,1)} fusion(bf16[4096,1536]{1,0:T(8,128)(2,1)} %all-gather.10.cloned.1.call-done, bf16[4096,640]{0,1:T(8,128)(2,1)} %get-tuple-element.92, bf16[4096,640]{0,1:T(8,128)(2,1)} %get-tuple-element.91), kind=kOutput, calls=%fused_computation.31 | convolution fusion | flops 16129064960 | bytes 27000832 | tf_op jit(solution)/shard_map/dot_general | solution.py:579
  819.0 4.7 all-to-all-start.3
  824.3 3.7 all-reduce.3.cloned.1.call-done
  828.0 2.5 dynamic-slice_bitcast_fusion
  830.5 104.7 %all-to-all-done.3 = bf16[8,192,1280]{2,1,0:T(8,128)(2,1)} async-done(((bf16[8,192,1280]{2,1,0:T(8,128)(2,1)}), bf16[8,192,1280]{2,1,0:T(8,128)(2,1)}, u32[]{:S(2)}, u32[]{:S(2)}) %all-to-all-start.3) | async-done | bytes 3932192 | tf_op jit(solution)/shard_map/all_to_all | solution.py:580
  935.2 3.9 all-to-all-start.2
  939.1 14.1 %fusion.25 = f32[640,1536]{1,0:T(8,128)} fusion(bf16[4096,640]{0,1:T(8,128)(2,1)} %get-tuple-element.93, bf16[4096,1664]{1,0:T(8,128)(2,1)} %all-gather.8.cloned.1.call-done), kind=kOutput, calls=%fused_computation.46 | convolution fusion | flops 8054046720 | bytes 21757952 | tf_op jit(solution)/shard_map/dot_general | solution.py:593
  953.2 7.4 copy.207
  960.6 4.0 convert_bitcast_fusion
  964.7 4.7 copy.208
  969.4 10.5 copy.209
  984.9 1.2 fusion.64
  986.1 140.8 %reduce-scatter.10.cloned.1.call-done = bf16[128,1536]{1,0:T(8,128)(2,1)} async-done(((bf16[4096,1536]{1,0:T(8,128)(2,1)}), bf16[128,1536]{1,0:T(8,128)(2,1)}) %reduce-scatter.10.cloned.1.call-update) | async-done | bytes 393232 | tf_op jit(solution)/shard_map/reduce_scatter | solution.py:575
  1127.0 2.9 fusion.63
  (209 shorter events, 24.4 us)
Async XLA Ops:
  8.0 29.4 %copy-start.47 = (s32[4]{0:T(128)S(1)}, s32[4]{0:T(128)}, u32[]{:S(2)}) copy-start(s32[4]{0:T(128)} %param.17) | copy-start | bytes 52
  8.0 49.6 %all-gather.16.cloned.1.call-start = ((), (), s32[]{:S(2)}) async-start(), calls=%async_computation.16 | async-start | bytes 2457600 | tf_op jit(solution)/shard_map/all_gather | solution.py:462
  36.6 83.3 %all-gather.14.cloned.1.call-start = ((), (), s32[]{:S(2)}) async-start(), calls=%async_computation.15 | async-start | bytes 3538944 | tf_op jit(solution)/shard_map/all_gather | solution.py:435
  37.3 228.8 %reduce-scatter.8.cloned.1.call-start = ((), (), s32[]{:S(2)}) async-start(), calls=%async_computation.8 | async-start | bytes 3538944 | tf_op jit(solution)/shard_map/reduce_scatter | solution.py:529
  60.9 64.7 %copy-start.13 = (bf16[8,4,48,640]{3,2,1,0:T(8,128)(2,1)}, bf16[8,4,48,640]{3,2,1,0:T(8,128)(2,1)S(1)}, u32[]{:S(2)}) copy-start(bf16[8,4,48,640]{3,2,1,0:T(8,128)(2,1)S(1)} %copy.184) | copy-start | bytes 5898244
  61.4 64.3 %copy-start.32 = (f32[1536]{0:T(1024)}, f32[1536]{0:T(1024)S(1)}, u32[]{:S(2)}) copy-start(f32[1536]{0:T(1024)S(1)} %get-tuple-element.82) | copy-start | bytes 18436
  61.4 597.1 %copy-start.29 = (f32[1536]{0:T(1024)}, f32[1536]{0:T(1024)S(1)}, u32[]{:S(2)}) copy-start(f32[1536]{0:T(1024)S(1)} %get-tuple-element.83) | copy-start | bytes 18436
  122.4 3.3 copy-start.40
  125.7 2.2 copy-start.20
  125.7 2.9 copy-start.5
  125.8 1.1 copy-start.11
  126.9 1.0 copy-start.15
  126.9 4.1 copy-start.25
  127.7 0.9 copy-start.9
  131.1 4.6 copy-start
  135.6 5.1 copy-start.34
  140.7 0.8 copy-start.27
  140.7 5.1 copy-start.39
  140.7 5.5 copy-start.38
  140.7 5.6 copy-start.18
  140.7 125.4 %copy-start.1 = (bf16[1,128,1536]{2,1,0:T(8,128)(2,1)S(1)}, bf16[1,128,1536]{2,1,0:T(8,128)(2,1)}, u32[]{:S(2)}) copy-start(bf16[1,128,1536]{2,1,0:T(8,128)(2,1)} %param.14) | copy-start | bytes 1179652
  145.8 154.4 %all-gather.8.cloned.1.call-start = ((), (), s32[]{:S(2)}) async-start(), calls=%async_computation.9 | async-start | bytes 14057472 | tf_op jit(solution)/shard_map/all_gather | solution.py:489
  147.3 286.0 %all-gather.10.cloned.1.call-start = ((), (), s32[]{:S(2)}) async-start(), calls=%async_computation.10 | async-start | bytes 12976128 | tf_op jit(solution)/shard_map/all_gather | solution.py:536
  267.3 391.1 %copy-start.36 = (f32[128]{0:T(128)}, f32[128]{0:T(128)S(1)}, u32[]{:S(2)}) copy-start(f32[128]{0:T(128)S(1)} %get-tuple-element.123) | copy-start | bytes 1540
  267.4 391.1 %copy-start.42 = (f32[128]{0:T(128)}, f32[128]{0:T(128)S(1)}, u32[]{:S(2)}) copy-start(f32[128]{0:T(128)S(1)} %get-tuple-element.122) | copy-start | bytes 1540
  291.0 142.3 %all-to-all-start.1 = ((bf16[8,192,1280]{2,1,0:T(8,128)(2,1)}), bf16[8,192,1280]{2,1,0:T(8,128)(2,1)}, u32[]{:S(2)}, u32[]{:S(2)}) async-start(bf16[8,192,1280]{2,1,0:T(8,128)(2,1)} %copy.195), calls=%async_computation.2 | async-start | bytes 7864320 | tf_op jit(solution)/shard_map/all_to_all | solution.py:499
  295.6 361.0 %reduce-scatter.12.cloned.1.call-start = ((), (), s32[]{:S(2)}) async-start(), calls=%async_computation.12 | async-start | bytes 12976128 | tf_op jit(solution)/shard_map/reduce_scatter | solution.py:571
  433.3 22.7 %copy-start.7 = (bf16[64,10,1536]{2,0,1:T(8,128)(2,1)S(1)}, bf16[64,10,1536]{2,0,1:T(8,128)(2,1)}, u32[]{:S(2)}) copy-start(bf16[64,10,1536]{2,0,1:T(8,128)(2,1)} %convert_element_type.229) | copy-start | bytes 5898244
  502.7 153.9 %copy-start.3 = (bf16[128,1536]{1,0:T(8,128)(2,1)S(1)}, bf16[128,1536]{1,0:T(8,128)(2,1)}, u32[]{:S(2)}) copy-start(bf16[128,1536]{1,0:T(8,128)(2,1)} %reduce-scatter.8.cloned.1.call-done) | copy-start | bytes 1179652
  502.7 220.5 %copy-start.6 = (pred[1024,1024]{0,1:T(8,128)(4,1)S(1)}, pred[1024,1024]{0,1:T(8,128)(4,1)}, u32[]{:S(2)}) copy-start(pred[1024,1024]{0,1:T(8,128)(4,1)} %fusion.23) | copy-start | bytes 3145732
  502.7 220.5 %copy-start.35 = (f32[3,1024]{1,0:T(4,128)S(1)}, f32[3,1024]{1,0:T(4,128)}, u32[]{:S(2)}) copy-start(f32[3,1024]{1,0:T(4,128)} %copy-done.34) | copy-start | bytes 36868
  502.8 216.9 %all-gather.12.cloned.1.call-start = ((), (), s32[]{:S(2)}) async-start(), calls=%async_computation.13 | async-start | bytes 3538944 | tf_op jit(solution)/shard_map/all_gather | solution.py:609
  658.4 64.8 %copy-start.44 = (f32[128]{0:T(128)}, f32[128]{0:T(128)S(1)}, u32[]{:S(2)}) copy-start(f32[128]{0:T(128)S(1)} %broadcast_multiply_fusion.2) | copy-start | bytes 1540
  660.6 167.4 %all-reduce.3.cloned.1.call-start = ((), (), s32[]{:S(2)}) async-start(), calls=%async_computation.17 | async-start | bytes 3932160
  723.3 17.3 %slice-start = ((s8[12582912]{0:T(1024)(128)(4,1)}), s8[4194304]{0:T(1024)(128)(4,1)S(1)}, s32[]{:S(2)}) async-start(s8[12582912]{0:T(1024)(128)(4,1)} %bitcast.267), calls=%async_computation.18 | async-start | bytes 8388608
  723.3 17.3 %slice-start.1 = ((s8[12582912]{0:T(1024)(128)(4,1)}), s8[4194304]{0:T(1024)(128)(4,1)S(1)}, s32[]{:S(2)}) async-start(s8[12582912]{0:T(1024)(128)(4,1)} %bitcast.267), calls=%async_computation.19 | async-start | bytes 8388608
  733.6 7.0 slice-start.2
  740.5 12.2 %copy-start.49 = (bf16[1024,64]{0,1:T(8,128)(2,1)}, bf16[1024,64]{0,1:T(8,128)(2,1)S(1)}, u32[]{:S(2)}) copy-start(bf16[1024,64]{0,1:T(8,128)(2,1)S(1)} %fusion.39) | copy-start | bytes 393220
  740.6 7.2 copy-start.23
  740.6 7.2 copy-start.26
  747.8 1.4 copy-start.10
  747.8 1.4 copy-start.12
  747.8 1.4 copy-start.16
  747.8 1.4 copy-start.24
  749.2 4.4 copy-start.21
  749.2 4.4 copy-start.33
  749.2 4.4 copy-start.41
  752.2 0.7 copy-start.28
  756.0 6.6 copy-start.14
  774.1 6.5 copy-start.8
  780.0 204.9 %reduce-scatter.14.cloned.1.call-start = ((), (), s32[]{:S(2)}) async-start(), calls=%async_computation.14 | async-start | bytes 3538944 | tf_op jit(solution)/shard_map/reduce_scatter | solution.py:644
  780.5 346.4 %reduce-scatter.10.cloned.1.call-start = ((), (), s32[]{:S(2)}) async-start(), calls=%async_computation.11 | async-start | bytes 12976128 | tf_op jit(solution)/shard_map/reduce_scatter | solution.py:575
  819.0 4.7 copy-start.48
  819.0 116.2 %all-to-all-start.3 = ((bf16[8,192,1280]{2,1,0:T(8,128)(2,1)}), bf16[8,192,1280]{2,1,0:T(8,128)(2,1)}, u32[]{:S(2)}, u32[]{:S(2)}) async-start(bf16[8,192,1280]{2,1,0:T(8,128)(2,1)} %bitcast.286), calls=%async_computation.7 | async-start | bytes 7864320 | tf_op jit(solution)/shard_map/all_to_all | solution.py:580
  935.2 44.7 %all-to-all-start.2 = ((bf16[8,48,640]{2,1,0:T(8,128)(2,1)}), bf16[8,48,640]{2,1,0:T(8,128)(2,1)S(1)}, u32[]{:S(2)}, u32[]{:S(2)}) async-start(bf16[8,48,640]{2,1,0:T(8,128)(2,1)} %dynamic-slice_bitcast_fusion), calls=%async_computation.6 | async-start | bytes 983040 | tf_op jit(solution)/shard_map/all_to_all | solution.py:664
  969.4 10.5 copy-start.46
  979.9 5.0 copy-start.2
  979.9 147.1 %copy-start.4 = (bf16[128,1536]{1,0:T(8,128)(2,1)S(1)}, bf16[128,1536]{1,0:T(8,128)(2,1)}, u32[]{:S(2)}) copy-start(bf16[128,1536]{1,0:T(8,128)(2,1)} %reduce-scatter.8.cloned.1.call-done) | copy-start | bytes 1179652
  979.9 147.1 %copy-start.17 = (bf16[128,1536]{1,0:T(8,128)(2,1)S(1)}, bf16[128,1536]{1,0:T(8,128)(2,1)}, u32[]{:S(2)}) copy-start(bf16[128,1536]{1,0:T(8,128)(2,1)} %reduce-scatter.12.cloned.1.call-done) | copy-start | bytes 1179652
  979.9 147.1 %copy-start.19 = (bf16[1,128,1536]{2,1,0:T(8,128)(2,1)S(1)}, bf16[1,128,1536]{2,1,0:T(8,128)(2,1)}, u32[]{:S(2)}) copy-start(bf16[1,128,1536]{2,1,0:T(8,128)(2,1)} %param.15) | copy-start | bytes 1179652
  979.9 147.0 %copy-start.30 = (f32[1536]{0:T(1024)S(1)}, f32[1536]{0:T(1024)}, u32[]{:S(2)}) copy-start(f32[1536]{0:T(1024)} %copy-done.29) | copy-start | bytes 18436
  979.9 147.0 %copy-start.37 = (f32[128]{0:T(128)S(1)}, f32[128]{0:T(128)}, u32[]{:S(2)}) copy-start(f32[128]{0:T(128)} %copy-done.36) | copy-start | bytes 1540
  979.9 147.0 %copy-start.43 = (f32[128]{0:T(128)S(1)}, f32[128]{0:T(128)}, u32[]{:S(2)}) copy-start(f32[128]{0:T(128)} %copy-done.42) | copy-start | bytes 1540
  979.9 147.0 %copy-start.45 = (f32[128]{0:T(128)S(1)}, f32[128]{0:T(128)}, u32[]{:S(2)}) copy-start(f32[128]{0:T(128)} %copy-done.44) | copy-start | bytes 1540
  (2 other events, 1.4 us)
Sparse Core Ops, SparseCore 0:
  36.7 20.8 all-gather.15
  59.8 60.0 all-gather.13
  145.9 120.1 reduce-scatter.7
  660.7 58.8 all-gather.11
  780.1 47.8 all-reduce.2
  831.5 135.2 reduce-scatter.13
  972.8 154.1 reduce-scatter.9
Sparse Core Ops, SparseCore 1:
  149.1 114.0 all-gather.7
  269.4 162.8 all-gather.9
  502.8 153.7 reduce-scatter.11
